TPU v7x, 128 devices: a whole 4x4x4 slice. The times are simulated.
128 devices in a mesh: segment: 4 (over x_lo, core), fsdp: 8 (over z, x_hi), dp: 4 (over y).
Axes of the slice: x: 4 (x_hi: 2, x_lo: 2; x = x_hi * 2 + x_lo), y: 4, z: 4, core: 2. Of those that a mesh axis runs over, the one named last changes fastest.
Arguments:
- inputs: bfloat16 [3, 64, 49, 2880], P(None, ('fsdp', 'dp')), may hold values from -6 to 6
- cotangent: bfloat16 [3, 64, 49, 2880], P(None, ('fsdp', 'dp')), may hold values from -0.119628906 to 0.119628906
- plan: int32 [3], replicated, may hold values from 0 to 2, each once
- weight: bfloat16 [4, 2880, 2880], P('segment', 'fsdp'), may hold values from -0.109375 to 0.109375
- squeeze: bfloat16 [4, 2880, 360], P('segment', 'fsdp'), may hold values from -0.109375 to 0.109375
- excite: bfloat16 [4, 2880, 360], P('segment', 'fsdp'), may hold values from -0.3125 to 0.3125
Outputs:
- grad_weight: float32 [4, 2880, 2880], P('segment', ('fsdp', 'dp'))
- grad_squeeze: float32 [4, 2880, 360], P('segment', ('fsdp', 'dp'))
- grad_excite: float32 [4, 2880, 360], P('segment', ('fsdp', 'dp'))
Inputs may be any that keep to these rules, and one draw needn't show every extreme that they name: plan names each of the 3 microbatches exactly once.
All inputs are finite; a program needn't handle non-finite values.
Results may differ from a plain program's by a relative error of at most 0.024.
Values may be sent and summed in bfloat16 or wider, within the bound.
A program may use at most 128 MiB of HBM per device.

v0:
```python
import jax
import jax.numpy as jnp
from jax import lax
from jax.sharding import PartitionSpec as P


def shifted(value, axis, steps):
    count = lax.axis_size(axis)
    leading, last = (max(0, -steps), min(count, count - steps))
    return lax.ppermute(value, axis, [(source, source + steps) for source in range(leading, last)])


def silu_slope(value):
    sigma = jax.nn.sigmoid(value)
    return sigma * (1.0 + value * (1.0 - sigma))


def contract_rows(left, right):
    return lax.dot_general(
        left, right, (((0,), (0,)), ((), ())), preferred_element_type=jnp.float32
    )


def contract_cols(left, right):
    return lax.dot_general(
        left, right, (((1,), (1,)), ((), ())), preferred_element_type=jnp.float32
    )


def project(images, matrix):
    flat = images.reshape(-1, images.shape[-1])
    result = jnp.dot(flat, matrix, preferred_element_type=jnp.float32)
    return result.reshape(images.shape[:-1] + (matrix.shape[1],))


def forward_block(images, matrix, squeeze_w, excite_w):
    pre = project(images, matrix)
    active_map = jax.nn.silu(pre).astype(jnp.bfloat16)
    pooled = jnp.mean(active_map.astype(jnp.float32), axis=1).astype(jnp.bfloat16)
    squeezed = jnp.dot(pooled, squeeze_w, preferred_element_type=jnp.float32)
    hidden = jax.nn.silu(squeezed).astype(jnp.bfloat16)
    gate = jax.nn.sigmoid(contract_cols(hidden, excite_w))
    output = (
        images.astype(jnp.float32) + active_map.astype(jnp.float32) * gate[:, None, :]
    ).astype(jnp.bfloat16)
    return (output, pre, pooled, squeezed, hidden, gate)


def backward_block(images, pre, squeezed, gate, upstream, matrix, squeeze_w, excite_w):
    active_map = jax.nn.silu(pre).astype(jnp.bfloat16)
    upper = upstream.astype(jnp.float32)
    d_act = upper * gate[:, None, :]
    d_gate = jnp.sum(upper * active_map.astype(jnp.float32), axis=1)
    d_excite = (d_gate * gate * (1.0 - gate)).astype(jnp.bfloat16)
    d_hidden = jnp.dot(d_excite, excite_w, preferred_element_type=jnp.float32)
    d_squeezed = (d_hidden * silu_slope(squeezed)).astype(jnp.bfloat16)
    d_pooled = contract_cols(d_squeezed, squeeze_w)
    d_act = d_act + d_pooled[:, None, :] / images.shape[1]
    d_pre = (d_act * silu_slope(pre)).astype(jnp.bfloat16)
    flat = d_pre.reshape(-1, d_pre.shape[-1])
    back = contract_cols(flat, matrix).reshape(images.shape)
    d_images = (upper + back).astype(jnp.bfloat16)
    return (d_excite, d_squeezed, d_pre, d_images)


def put_slot(store, position, value, active):
    current = lax.dynamic_index_in_dim(store, position, 0, keepdims=False)
    return lax.dynamic_update_index_in_dim(store, jnp.where(active, value, current), position, 0)


def take_slot(store, position):
    return lax.dynamic_index_in_dim(store, position, 0, keepdims=False)


def on_device(inputs, cotangent, plan, weight, squeeze, excite):
    full_w, full_s, full_e = (
        lax.all_gather(weight[0], "fsdp", axis=0, tiled=True),
        lax.all_gather(squeeze[0], "fsdp", axis=0, tiled=True),
        lax.all_gather(excite[0], "fsdp", axis=0, tiled=True),
    )
    sections = lax.axis_size("segment")
    segment_id = lax.axis_index("segment")
    ordered = inputs[plan]
    micro, images, pixels, width = ordered.shape
    hidden_width = full_s.shape[1]
    steps_total = micro + sections - 1
    store_in = jnp.zeros((micro, images, pixels, width), jnp.bfloat16)
    store_pre = jnp.zeros((micro, images, pixels, width), jnp.float32)
    store_pool = jnp.zeros((micro, images, width), jnp.bfloat16)
    store_sq = jnp.zeros((micro, images, hidden_width), jnp.float32)
    store_hid = jnp.zeros((micro, images, hidden_width), jnp.bfloat16)
    store_gate = jnp.zeros((micro, images, width), jnp.float32)
    incoming = jnp.zeros((images, pixels, width), jnp.bfloat16)
    for step in range(steps_total):
        slot_now = step - segment_id
        active = (slot_now >= 0) & (slot_now < micro)
        position = jnp.clip(slot_now, 0, micro - 1)
        first_in = ordered[min(step, micro - 1)]
        images_in = jnp.where(segment_id == 0, first_in, incoming)
        output, pre, pooled, squeezed, hidden, gate = forward_block(
            images_in, full_w, full_s, full_e
        )
        store_in = put_slot(store_in, position, images_in, active)
        store_pre = put_slot(store_pre, position, pre, active)
        store_pool = put_slot(store_pool, position, pooled, active)
        store_sq = put_slot(store_sq, position, squeezed, active)
        store_hid = put_slot(store_hid, position, hidden, active)
        store_gate = put_slot(store_gate, position, gate, active)
        if step < steps_total - 1:
            incoming = shifted(output, "segment", 1)
    store_dpre = jnp.zeros((micro, images, pixels, width), jnp.bfloat16)
    store_dsq = jnp.zeros((micro, images, hidden_width), jnp.bfloat16)
    store_dex = jnp.zeros((micro, images, width), jnp.bfloat16)
    incoming_grad = jnp.zeros((images, pixels, width), jnp.bfloat16)
    for step in range(steps_total):
        slot_now = micro - 1 - step + (sections - 1 - segment_id)
        active = (slot_now >= 0) & (slot_now < micro)
        position = jnp.clip(slot_now, 0, micro - 1)
        last_in = cotangent[max(micro - 1 - step, 0)]
        upstream = jnp.where(segment_id == sections - 1, last_in, incoming_grad)
        images_in = take_slot(store_in, position)
        pre = take_slot(store_pre, position)
        squeezed = take_slot(store_sq, position)
        gate = take_slot(store_gate, position)
        d_excite, d_squeezed, d_pre, d_images = backward_block(
            images_in, pre, squeezed, gate, upstream, full_w, full_s, full_e
        )
        store_dpre = put_slot(store_dpre, position, d_pre, active)
        store_dsq = put_slot(store_dsq, position, d_squeezed, active)
        store_dex = put_slot(store_dex, position, d_excite, active)
        if step < steps_total - 1:
            incoming_grad = shifted(d_images, "segment", -1)
    flat_in = store_in.reshape(-1, width)
    flat_dpre = store_dpre.reshape(-1, width)
    grad_s = contract_rows(store_pool.reshape(-1, width), store_dsq.reshape(-1, hidden_width))
    grad_e = contract_rows(store_dex.reshape(-1, width), store_hid.reshape(-1, hidden_width))
    grad_w = contract_rows(flat_in, flat_dpre)
    shard_w, shard_s, shard_e = (
        lax.psum_scatter(
            grad_w.astype(jnp.bfloat16), ("fsdp", "dp"), scatter_dimension=0, tiled=True
        ).astype(jnp.float32),
        lax.psum_scatter(
            grad_s.astype(jnp.bfloat16), ("fsdp", "dp"), scatter_dimension=0, tiled=True
        ).astype(jnp.float32),
        lax.psum_scatter(
            grad_e.astype(jnp.bfloat16), ("fsdp", "dp"), scatter_dimension=0, tiled=True
        ).astype(jnp.float32),
    )
    return (shard_w[None], shard_s[None], shard_e[None])


def solution(mesh):
    placed = (
        P(None, ("fsdp", "dp"), None, None),
        P(None, ("fsdp", "dp"), None, None),
        P(),
        P("segment", "fsdp", None),
        P("segment", "fsdp", None),
        P("segment", "fsdp", None),
    )
    return jax.shard_map(
        on_device,
        mesh=mesh,
        in_specs=placed,
        out_specs=(
            P("segment", ("fsdp", "dp"), None),
            P("segment", ("fsdp", "dp"), None),
            P("segment", ("fsdp", "dp"), None),
        ),
        check_vma=False,
    )
```

profile of v0, /device:TPU:42, one launch (start us, length us, event | category | flops | bytes accessed | tf_op | source)
XLA Modules:
  0.0 888.6 jit_solution(14493084215448957604)
XLA Ops:
  9.5 6.0 gather_fusion
  15.4 3.4 fusion.357
  21.3 2.1 constant_dynamic-slice_fusion.56
  23.4 2.3 fusion.356
  25.6 168.4 %all-gather.7.cloned.1.call-done = bf16[1,2880,2880]{2,1,0:T(8,128)(2,1)} async-done(((bf16[1,360,2880]{2,1,0:T(8,128)(2,1)}), bf16[1,2880,2880]{2,1,0:T(8,128)(2,1)}) %all-gather.7.cloned.1.call-update) | async-done | bytes 16588816 | tf_op jit(solution)/shard_map/all_gather | solution.py:77
  194.0 9.7 %convert_reduce_fusion.4 = (f32[2,2880]{1,0:T(2,128)S(1)}, bf16[2,49,2880]{2,1,0:T(8,128)(2,1)S(1)}, f32[2,49,2880]{2,1,0:T(8,128)}) fusion(bf16[1,2880,2880]{2,1,0:T(8,128)(2,1)} %all-gather.7.cloned.1.call-done, bf16[1,2,49,2880]{3,1,2,0:T(2,128)(2,1)S(1)} %get-tuple-element.33, pred[]{:T(512)S(6)} %eq.4), kind=kOutput, calls=%fused_computation.130 | convolution fusion | flops 1627954560 | bytes 18869760 | tf_op jit(solution)/shard_map/dot_general | solution.py:32
  203.7 45.0 %all-gather.9.cloned.1.call-done = bf16[1,2880,360]{2,1,0:T(8,128)(2,1)} async-done(((bf16[1,360,360]{2,1,0:T(8,128)(2,1)}), bf16[1,2880,360]{2,1,0:T(8,128)(2,1)}) %all-gather.9.cloned.1.call-update) | async-done | bytes 2073616 | tf_op jit(solution)/shard_map/all_gather | solution.py:78
  248.7 2.0 constant_dynamic-update-slice_fusion.29
  250.7 52.7 %all-gather.11.cloned.1.call-done = bf16[1,2880,360]{2,1,0:T(8,128)(2,1)} async-done(((bf16[1,360,360]{2,1,0:T(8,128)(2,1)}), bf16[1,2880,360]{2,1,0:T(8,128)(2,1)}) %all-gather.11.cloned.1.call-update) | async-done | bytes 2073616 | tf_op jit(solution)/shard_map/all_gather | solution.py:79
  303.4 2.3 constant_dynamic-update-slice_fusion.34
  306.4 2.1 collective-permute-start
  310.2 7.3 collective-permute-done
  317.5 8.8 convert_reduce_fusion.3
  329.7 1.9 collective-permute-start.1
  335.2 5.6 collective-permute-done.1
  340.8 4.0 convert_reduce_fusion.2
  346.7 2.1 collective-permute-start.2
  351.4 6.3 collective-permute-done.2
  357.8 4.0 convert_reduce_fusion.1
  363.7 1.9 collective-permute-start.3
  368.2 6.6 collective-permute-done.3
  374.7 2.9 convert_reduce_fusion
  379.9 2.3 collective-permute-start.4
  383.3 2.0 constant_dynamic-slice_fusion.52
  385.3 5.7 collective-permute-done.4
  391.0 5.0 bitcast_dynamic-update-slice_fusion
  396.0 3.2 fusion.126
  404.0 12.6 %fusion.54 = bf16[2,49,2880]{2,1,0:T(8,128)(2,1)} fusion(bf16[1,2880,2880]{2,1,0:T(8,128)(2,1)} %all-gather.7.cloned.1.call-done, f32[3,2,49,2880]{3,2,1,0:T(8,128)} %copy-done.9, s32[]{:T(128)S(6)} %min.30, f32[2,2880]{1,0:T(2,128)} %convolution_multiply_fusion.5, f32[2,2880]{1,0:T(2,128)} %copy-done.39, bf16[1,2,49,2880]{3,1,2,0:T(2,128)(2,1)} %get-tuple-element.30, ...), kind=kOutput, calls=%fused_computation.37 | convolution fusion | flops 1630500480 | bytes 20043520 | tf_op jit(solution)/shard_map/dot_general | solution.py:25
  418.2 2.1 collective-permute-start.5
  421.2 2.1 select_dynamic-update-slice_fusion
  424.8 2.2 bitcast_dynamic-update-slice_fusion.11
  427.4 2.2 fusion.140
  431.9 12.4 %fusion.51 = bf16[2,49,2880]{2,1,0:T(8,128)(2,1)} fusion(bf16[1,2880,2880]{2,1,0:T(8,128)(2,1)} %all-gather.7.cloned.1.call-done, bf16[2,49,2880]{2,0,1:T(2,128)(2,1)} %copy-done.24, bf16[1,2,49,2880]{3,1,2,0:T(2,128)(2,1)S(1)} %copy-done.14, pred[]{:T(512)S(6)} %eq.5, f32[3,2,49,2880]{3,2,1,0:T(8,128)} %copy-done.9, s32[]{:T(128)S(6)} %min.29, ...), kind=kOutput, calls=%fused_computation.36 | convolution fusion | flops 1630500480 | bytes 21197568 | tf_op jit(solution)/shard_map/dot_general | solution.py:25
  446.0 3.8 collective-permute-start.6
  450.5 3.0 bitcast_dynamic-update-slice_fusion.10
  453.5 2.0 constant_dynamic-slice_fusion.29
  456.8 2.0 fusion.144
  461.2 12.2 %fusion.48 = bf16[2,49,2880]{2,1,0:T(8,128)(2,1)} fusion(bf16[1,2880,2880]{2,1,0:T(8,128)(2,1)} %all-gather.7.cloned.1.call-done, bf16[2,49,2880]{2,0,1:T(2,128)(2,1)S(1)} %copy-done.27, bf16[1,2,49,2880]{3,1,2,0:T(2,128)(2,1)S(1)} %get-tuple-element.28, pred[]{:T(512)S(6)} %eq.5, f32[3,2,49,2880]{3,2,1,0:T(8,128)} %copy-done.9, s32[]{:T(128)S(6)} %min.28, ...), kind=kOutput, calls=%fused_computation.35 | convolution fusion | flops 1630500480 | bytes 21197568 | tf_op jit(solution)/shard_map/dot_general | solution.py:25
  475.0 4.1 collective-permute-start.7
  479.7 3.0 bitcast_dynamic-update-slice_fusion.9
  482.7 2.0 constant_dynamic-slice_fusion.26
  486.1 2.0 fusion.148
  490.4 12.2 %fusion.45 = bf16[2,49,2880]{2,1,0:T(8,128)(2,1)} fusion(bf16[1,2880,2880]{2,1,0:T(8,128)(2,1)} %all-gather.7.cloned.1.call-done, bf16[2,49,2880]{2,0,1:T(2,128)(2,1)S(1)} %copy-done.31, bf16[1,2,49,2880]{3,1,2,0:T(2,128)(2,1)S(1)} %get-tuple-element.28, pred[]{:T(512)S(6)} %eq.5, f32[3,2,49,2880]{3,2,1,0:T(8,128)} %copy-done.9, s32[]{:T(128)S(6)} %min.27, ...), kind=kOutput, calls=%fused_computation.34 | convolution fusion | flops 1630500480 | bytes 21197568 | tf_op jit(solution)/shard_map/dot_general | solution.py:25
  504.2 4.3 collective-permute-start.8
  509.2 2.9 bitcast_dynamic-update-slice_fusion.8
  512.1 2.0 constant_dynamic-slice_fusion.23
  515.3 2.0 fusion.152
  519.6 12.2 %fusion.42 = bf16[2,49,2880]{2,1,0:T(8,128)(2,1)} fusion(bf16[1,2880,2880]{2,1,0:T(8,128)(2,1)} %all-gather.7.cloned.1.call-done, bf16[2,49,2880]{2,0,1:T(2,128)(2,1)S(1)} %collective-permute-done.8, bf16[1,2,49,2880]{3,1,2,0:T(2,128)(2,1)S(1)} %get-tuple-element.28, pred[]{:T(512)S(6)} %eq.5, f32[3,2,49,2880]{3,2,1,0:T(8,128)} %copy-done.9, s32[]{:T(128)S(6)} %min.26, ...), kind=kOutput, calls=%fused_computation.33 | convolution fusion | flops 1630500480 | bytes 21197568 | tf_op jit(solution)/shard_map/dot_general | solution.py:25
  533.4 4.0 collective-permute-start.9
  538.1 3.1 bitcast_dynamic-update-slice_fusion.7
  542.4 2.1 collective-permute-done.9
  545.1 2.2 fusion.26
  548.2 2.9 fusion.25
  553.4 13.9 %bitcast_convert_fusion = bf16[2880,2880]{1,0:T(8,128)(2,1)} fusion(bf16[3,2,49,2880]{3,2,1,0:T(8,128)(2,1)} %bitcast_dynamic-update-slice_fusion.11, bf16[3,2,49,2880]{3,2,1,0:T(8,128)(2,1)S(1)} %bitcast_dynamic-update-slice_fusion.6), kind=kOutput, calls=%fused_computation.1 | convolution fusion | flops 4885401600 | bytes 19975680 | tf_op jit(solution)/shard_map/dot_general | solution.py:19
  567.3 249.8 %fusion.355 = (bf16[96,2880]{1,0:T(8,128)(2,1)S(1)}, bf16[96,360]{1,0:T(8,128)(2,1)S(1)}, bf16[96,360]{1,0:T(8,128)(2,1)S(1)}) fusion(bf16[2880,2880]{1,0:T(8,128)(2,1)} %bitcast_convert_fusion, bf16[2880,360]{1,0:T(8,128)(2,1)} %fusion.25, bf16[2880,360]{1,0:T(8,128)(2,1)S(1)} %copy-done.33), kind=kCustom, calls=%all-reduce-scatter.3 | all-reduce-scatter fusion | flops 11059201 | bytes 21427712
  817.1 1.9 collective-permute-start.10
  819.2 5.6 collective-permute-start.11
  824.8 1.9 collective-permute-start.14
  826.8 2.5 collective-permute-start.15
  830.6 7.7 collective-permute-start.12
  838.2 18.1 %collective-permute-done.15 = bf16[90,360]{1,0:T(8,128)(2,1)S(1)} collective-permute-done((bf16[90,360]{1,0:T(8,128)(2,1)S(1)}, bf16[90,360]{1,0:T(8,128)(2,1)S(1)}, u32[]{:S(2)}, u32[]{:S(2)}) %collective-permute-start.15) | collective-permute-done | bytes 64832
  859.8 7.6 collective-permute-done.13
  868.9 9.5 %concatenate = bf16[282,2880]{1,0:T(8,128)(2,1)} concatenate(bf16[90,2880]{1,0:T(8,128)(2,1)S(1)} %collective-permute-done.11, bf16[96,2880]{1,0:T(8,128)(2,1)S(1)} %collective-permute-done.10, bf16[96,2880]{1,0:T(8,128)(2,1)S(1)} %get-tuple-element.15), dimensions={0} | concatenate | bytes 3248640
  879.8 2.1 copy.68
  (229 shorter events, 69.6 us)
Async XLA Ops:
  7.2 2.3 copy-start
  7.2 2.2 copy-start.45
  7.2 186.8 %all-gather.7.cloned.1.call-start = ((), (), s32[]{:S(2)}) async-start(), calls=%async_computation | async-start | bytes 19077120 | tf_op jit(solution)/shard_map/all_gather | solution.py:77
  7.9 240.7 %all-gather.9.cloned.1.call-start = ((), (), s32[]{:S(2)}) async-start(), calls=%async_computation.1 | async-start | bytes 2488320 | tf_op jit(solution)/shard_map/all_gather | solution.py:78
  8.7 294.7 %all-gather.11.cloned.1.call-start = ((), (), s32[]{:S(2)}) async-start(), calls=%async_computation.2 | async-start | bytes 2488320 | tf_op jit(solution)/shard_map/all_gather | solution.py:79
  20.3 3.1 copy-start.34
  306.4 11.1 %collective-permute-start = (bf16[2,49,2880]{2,0,1:T(2,128)(2,1)S(1)}, bf16[2,49,2880]{2,0,1:T(2,128)(2,1)S(1)}, u32[]{:S(2)}, u32[]{:S(2)}) collective-permute-start(bf16[2,49,2880]{2,0,1:T(2,128)(2,1)S(1)} %copy.44), channel_id=1, source_target_pairs={{0,32},{32,64},{64,96},{1,33},{33,65},{65,97},{2,34},{34,66},{66,9... | collective-permute-start | bytes 1693448 | tf_op jit(solution)/shard_map/ppermute | solution.py:10
  310.0 7.5 copy-start.17
  317.5 8.9 copy-start.2
  317.5 23.2 %slice-start = ((s8[16957440]{0:T(1024)(128)(4,1)}), s8[4194304]{0:T(1024)(128)(4,1)S(1)}, s32[]{:S(2)}) async-start(s8[16957440]{0:T(1024)(128)(4,1)} %bitcast.890), calls=%async_computation.3 | async-start | bytes 8388608
  317.5 23.2 %slice-start.1 = ((s8[16957440]{0:T(1024)(128)(4,1)}), s8[4194304]{0:T(1024)(128)(4,1)S(1)}, s32[]{:S(2)}) async-start(s8[16957440]{0:T(1024)(128)(4,1)} %bitcast.890), calls=%async_computation.4 | async-start | bytes 8388608
  317.5 23.2 %slice-start.2 = ((s8[16957440]{0:T(1024)(128)(4,1)}), s8[4194304]{0:T(1024)(128)(4,1)S(1)}, s32[]{:S(2)}) async-start(s8[16957440]{0:T(1024)(128)(4,1)} %bitcast.890), calls=%async_computation.5 | async-start | bytes 8388608
  326.3 1.9 copy-start.3
  326.4 14.4 %slice-start.3 = ((s8[16957440]{0:T(1024)(128)(4,1)}), s8[4194304]{0:T(1024)(128)(4,1)S(1)}, s32[]{:S(2)}) async-start(s8[16957440]{0:T(1024)(128)(4,1)} %bitcast.890), calls=%async_computation.6 | async-start | bytes 8388608
  329.7 11.1 %collective-permute-start.1 = (bf16[2,49,2880]{2,0,1:T(2,128)(2,1)S(1)}, bf16[2,49,2880]{2,0,1:T(2,128)(2,1)S(1)}, u32[]{:S(2)}, u32[]{:S(2)}) collective-permute-start(bf16[2,49,2880]{2,0,1:T(2,128)(2,1)S(1)} %copy.47), channel_id=1, source_target_pairs={{0,32},{32,64},{64,96},{1,33},{33,65},{65,97},{2,34},{34,66},{66,9... | collective-permute-start | bytes 1693448 | tf_op jit(solution)/shard_map/ppermute | solution.py:10
  331.6 9.1 %slice-start.4 = ((s8[16957440]{0:T(1024)(128)(4,1)}), s8[180224]{0:T(1024)(128)(4,1)S(1)}, s32[]{:S(2)}) async-start(s8[16957440]{0:T(1024)(128)(4,1)} %bitcast.890), calls=%async_computation.7 | async-start | bytes 360448
  345.9 2.9 copy-start.36
  346.7 11.1 %collective-permute-start.2 = (bf16[2,49,2880]{2,0,1:T(2,128)(2,1)S(1)}, bf16[2,49,2880]{2,0,1:T(2,128)(2,1)S(1)}, u32[]{:S(2)}, u32[]{:S(2)}) collective-permute-start(bf16[2,49,2880]{2,0,1:T(2,128)(2,1)S(1)} %copy.49), channel_id=1, source_target_pairs={{0,32},{32,64},{64,96},{1,33},{33,65},{65,97},{2,34},{34,66},{66,9... | collective-permute-start | bytes 1693448 | tf_op jit(solution)/shard_map/ppermute | solution.py:10
  362.9 2.7 copy-start.37
  363.7 11.1 %collective-permute-start.3 = (bf16[2,49,2880]{2,0,1:T(2,128)(2,1)S(1)}, bf16[2,49,2880]{2,0,1:T(2,128)(2,1)S(1)}, u32[]{:S(2)}, u32[]{:S(2)}) collective-permute-start(bf16[2,49,2880]{2,0,1:T(2,128)(2,1)S(1)} %copy.51), channel_id=1, source_target_pairs={{0,32},{32,64},{64,96},{1,33},{33,65},{65,97},{2,34},{34,66},{66,9... | collective-permute-start | bytes 1693448 | tf_op jit(solution)/shard_map/ppermute | solution.py:10
  379.9 11.2 %collective-permute-start.4 = (bf16[2,49,2880]{2,0,1:T(2,128)(2,1)S(1)}, bf16[2,49,2880]{2,0,1:T(2,128)(2,1)}, u32[]{:S(2)}, u32[]{:S(2)}) collective-permute-start(bf16[2,49,2880]{2,0,1:T(2,128)(2,1)S(1)} %copy.53), channel_id=1, source_target_pairs={{0,32},{32,64},{64,96},{1,33},{33,65},{65,97},{2,34},{34,66},{66,9... | collective-permute-start | bytes 1693448 | tf_op jit(solution)/shard_map/ppermute | solution.py:10
  385.3 10.7 %copy-start.15 = (bf16[1,2,49,2880]{3,1,2,0:T(2,128)(2,1)S(1)}, bf16[1,2,49,2880]{3,1,2,0:T(2,128)(2,1)}, u32[]{:S(2)}) copy-start(bf16[1,2,49,2880]{3,1,2,0:T(2,128)(2,1)} %get-tuple-element.30) | copy-start | bytes 1693444
  396.0 5.1 copy-start.9
  401.1 1.7 copy-start.39
  416.6 4.5 copy-start.16
  416.6 4.6 copy-start.40
  416.6 4.6 copy-start.41
  418.2 9.2 %collective-permute-start.5 = (bf16[2,49,2880]{2,0,1:T(2,128)(2,1)S(1)}, bf16[2,49,2880]{2,0,1:T(2,128)(2,1)S(1)}, u32[]{:S(2)}, u32[]{:S(2)}) collective-permute-start(bf16[2,49,2880]{2,0,1:T(2,128)(2,1)S(1)} %copy.57), channel_id=1, source_target_pairs={{32,0},{64,32},{96,64},{33,1},{65,33},{97,65},{34,2},{66,34},{98,6... | collective-permute-start | bytes 1693448 | tf_op jit(solution)/shard_map/ppermute | solution.py:10
  421.2 3.6 copy-start.19
  423.3 1.5 copy-start.11
  424.8 2.6 copy-start.13
  427.0 2.6 copy-start.4
  427.4 3.2 copy-start.24
  444.3 6.2 copy-start.20
  444.3 6.2 copy-start.25
  446.0 10.9 %collective-permute-start.6 = (bf16[2,49,2880]{2,0,1:T(2,128)(2,1)S(1)}, bf16[2,49,2880]{2,0,1:T(2,128)(2,1)S(1)}, u32[]{:S(2)}, u32[]{:S(2)}) collective-permute-start(bf16[2,49,2880]{2,0,1:T(2,128)(2,1)S(1)} %copy.60), channel_id=1, source_target_pairs={{32,0},{64,32},{96,64},{33,1},{65,33},{97,65},{34,2},{66,34},{98,6... | collective-permute-start | bytes 1693448 | tf_op jit(solution)/shard_map/ppermute | solution.py:10
  455.5 3.4 copy-start.5
  456.8 3.0 copy-start.26
  473.4 6.4 copy-start.21
  475.0 11.1 %collective-permute-start.7 = (bf16[2,49,2880]{2,0,1:T(2,128)(2,1)S(1)}, bf16[2,49,2880]{2,0,1:T(2,128)(2,1)S(1)}, u32[]{:S(2)}, u32[]{:S(2)}) collective-permute-start(bf16[2,49,2880]{2,0,1:T(2,128)(2,1)S(1)} %copy.62), channel_id=1, source_target_pairs={{32,0},{64,32},{96,64},{33,1},{65,33},{97,65},{34,2},{66,34},{98,6... | collective-permute-start | bytes 1693448 | tf_op jit(solution)/shard_map/ppermute | solution.py:10
  484.7 3.4 copy-start.6
  486.1 3.0 copy-start.30
  502.6 6.6 copy-start.23
  502.6 6.6 copy-start.32
  504.2 11.1 %collective-permute-start.8 = (bf16[2,49,2880]{2,0,1:T(2,128)(2,1)S(1)}, bf16[2,49,2880]{2,0,1:T(2,128)(2,1)S(1)}, u32[]{:S(2)}, u32[]{:S(2)}) collective-permute-start(bf16[2,49,2880]{2,0,1:T(2,128)(2,1)S(1)} %copy.64), channel_id=1, source_target_pairs={{32,0},{64,32},{96,64},{33,1},{65,33},{97,65},{34,2},{66,34},{98,6... | collective-permute-start | bytes 1693448 | tf_op jit(solution)/shard_map/ppermute | solution.py:10
  514.1 3.2 copy-start.7
  515.3 4.3 copy-start.28
  531.8 6.3 copy-start.22
  531.8 6.3 copy-start.29
  533.4 11.1 %collective-permute-start.9 = (bf16[2,49,2880]{2,0,1:T(2,128)(2,1)S(1)}, bf16[2,49,2880]{2,0,1:T(2,128)(2,1)S(1)}, u32[]{:S(2)}, u32[]{:S(2)}) collective-permute-start(bf16[2,49,2880]{2,0,1:T(2,128)(2,1)S(1)} %copy.66), channel_id=1, source_target_pairs={{32,0},{64,32},{96,64},{33,1},{65,33},{97,65},{34,2},{66,34},{98,6... | collective-permute-start | bytes 1693448 | tf_op jit(solution)/shard_map/ppermute | solution.py:10
  538.1 6.4 copy-start.10
  542.3 2.7 copy-start.43
  545.0 2.2 copy-start.8
  545.0 2.2 copy-start.38
  551.1 1.5 copy-start.12
  553.4 13.9 %copy-start.33 = (bf16[2880,360]{1,0:T(8,128)(2,1)S(1)}, bf16[2880,360]{1,0:T(8,128)(2,1)}, u32[]{:S(2)}) copy-start(bf16[2880,360]{1,0:T(8,128)(2,1)} %fusion.26) | copy-start | bytes 6220804
  567.3 262.0 %copy-start.44 = (u32[128]{0:T(128)S(1)}, u32[128]{0:T(128)}, u32[]{:S(2)}) copy-start(u32[128]{0:T(128)} %constant.371) | copy-start | bytes 1540
  817.1 51.8 %collective-permute-start.10 = (bf16[96,2880]{1,0:T(8,128)(2,1)S(1)}, bf16[96,2880]{1,0:T(8,128)(2,1)S(1)}, u32[]{:S(2)}, u32[]{:S(2)}) collective-permute-start(bf16[96,2880]{1,0:T(8,128)(2,1)S(1)} %get-tuple-element.15), channel_id=1, source_target_pairs={{0,1},{1,2},{2,3},{3,4},{4,5},{5,6},{6,7},{7,8},{8,9},{9,10},{10,1... | collective-permute-start | bytes 1658888
  819.2 49.7 %collective-permute-start.11 = (bf16[90,2880]{1,0:T(8,128)(2,1)S(1)}, bf16[90,2880]{1,0:T(8,128)(2,1)S(1)}, u32[]{:S(2)}, u32[]{:S(2)}) collective-permute-start(bf16[90,2880]{1,0:T(8,128)(2,1)S(1)} %slice.35), channel_id=1, source_target_pairs={{0,2},{1,3},{2,4},{3,5},{4,6},{5,7},{6,8},{7,9},{8,10},{9,11},{10,... | collective-permute-start | bytes 1555208
  824.8 33.4 %collective-permute-start.14 = (bf16[96,360]{1,0:T(8,128)(2,1)S(1)}, bf16[96,360]{1,0:T(8,128)(2,1)S(1)}, u32[]{:S(2)}, u32[]{:S(2)}) collective-permute-start(bf16[96,360]{1,0:T(8,128)(2,1)S(1)} %get-tuple-element.17), channel_id=1, source_target_pairs={{0,1},{1,2},{2,3},{3,4},{4,5},{5,6},{6,7},{7,8},{8,9},{9,10},{10,1... | collective-permute-start | bytes 207368
  826.8 29.6 %collective-permute-start.15 = (bf16[90,360]{1,0:T(8,128)(2,1)S(1)}, bf16[90,360]{1,0:T(8,128)(2,1)S(1)}, u32[]{:S(2)}, u32[]{:S(2)}) collective-permute-start(bf16[90,360]{1,0:T(8,128)(2,1)S(1)} %slice.37), channel_id=1, source_target_pairs={{0,2},{1,3},{2,4},{3,5},{4,6},{5,7},{6,8},{7,9},{8,10},{9,11},{10,... | collective-permute-start | bytes 194408
  830.6 36.8 %collective-permute-start.12 = (bf16[96,360]{1,0:T(8,128)(2,1)S(1)}, bf16[96,360]{1,0:T(8,128)(2,1)S(1)}, u32[]{:S(2)}, u32[]{:S(2)}) collective-permute-start(bf16[96,360]{1,0:T(8,128)(2,1)S(1)} %get-tuple-element.16), channel_id=1, source_target_pairs={{0,1},{1,2},{2,3},{3,4},{4,5},{5,6},{6,7},{7,8},{8,9},{9,10},{10,1... | collective-permute-start | bytes 207368
  856.3 11.0 %collective-permute-start.13 = (bf16[90,360]{1,0:T(8,128)(2,1)S(1)}, bf16[90,360]{1,0:T(8,128)(2,1)S(1)}, u32[]{:S(2)}, u32[]{:S(2)}) collective-permute-start(bf16[90,360]{1,0:T(8,128)(2,1)S(1)} %slice.36), channel_id=1, source_target_pairs={{0,2},{1,3},{2,4},{3,5},{4,6},{5,7},{6,8},{7,9},{8,10},{9,11},{10,... | collective-permute-start | bytes 194408
  878.5 3.4 copy-start.1
  (6 other events, 7.8 us)
Sparse Core Ops, SparseCore 0:
  10.3 183.6 all-gather.6
  196.3 52.3 all-gather.8
  251.0 52.3 all-gather.10
where the time goes:
time: 898 us; the launch traced here: 889 us
  waiting for transfers between devices  332 us (37%)
  blocking collectives  250 us (28%)
  matrix products  138 us (15%)
  local copies, waits for them, and re-layouts  65.1 us (7%)
  starting transfers between devices  50.3 us (6%)
  other arithmetic  38.5 us (4%)
  between operations  15.5 us (2%)
    unnamed x1, blocking collectives  250 us
    all_gather x1, waiting for transfers between devices, on_device(): lax.all_gather(weight[0], 'fsdp', axis=0, tiled=True)  168 us
    dot_general x17, matrix products, contract_cols(): lax.dot_general(left, right, (((1,), (1,)), ((), ())), preferred_element_...  74.6 us
    all_gather x1, waiting for transfers between devices, on_device(): lax.all_gather(excite[0], 'fsdp', axis=0, tiled=True)  52.7 us
    all_gather x1, waiting for transfers between devices, on_device(): lax.all_gather(squeeze[0], 'fsdp', axis=0, tiled=True)  45 us
    ppermute x10, waiting for transfers between devices, shifted(): lax.ppermute(value, axis, [(source, source + steps) for source in range(l...  37.8 us
    dot_general x6, matrix products, project(): result = jnp.dot(flat, matrix, preferred_element_type=jnp.float32)  34.4 us
    ppermute x10, starting transfers between devices, shifted(): lax.ppermute(value, axis, [(source, source + steps) for source in range(l...  28.7 us
  transfers between devices with their start and end apart: 19, of which 15 were waited for; matrix products, arithmetic and copies ran while one was open for 8% of the time, Pallas kernels for 0%

commit v1 on v0

--- a/solution.py
+++ b/solution.py
@@ -74,7 +74,9 @@
 
 def on_device(inputs, cotangent, plan, weight, squeeze, excite):
     full_w, full_s, full_e = (
-        lax.all_gather(weight[0], "fsdp", axis=0, tiled=True),
+        jnp.concatenate(
+            lax.all_to_all(jnp.stack([weight[0]] * lax.axis_size("fsdp")), "fsdp", 0, 0), axis=0
+        ),
         lax.all_gather(squeeze[0], "fsdp", axis=0, tiled=True),
         lax.all_gather(excite[0], "fsdp", axis=0, tiled=True),
     )

time: 898 us -> 891 us (level)
  waiting for transfers between devices: 332 us -> 295 us
  matrix products: 138 us -> 157 us
    all_to_all x0 -> x1, waiting for transfers between devices: none -> 183 us  [on_device(): lax.all_to_all(jnp.stack([weight[0]] * lax.axis_size('fsdp')), 'fsdp', 0, 0)]
    all_gather x1 -> x0, waiting for transfers between devices: 168 us -> none  [on_device(): lax.all_gather(weight[0], 'fsdp', axis=0, tiled=True)]
    all_gather x1, waiting for transfers between devices: 45 us -> 0.02 us  [on_device(): lax.all_gather(squeeze[0], 'fsdp', axis=0, tiled=True)]
    dot_general x6, matrix products: 34.4 us -> 53.2 us  [project(): result = jnp.dot(flat, matrix, preferred_element_type=jnp.float32)]
    unnamed x9 -> x8, waiting for transfers between devices: 27.7 us -> 27 us
    unnamed x112 -> x100, local copies, waits for them, and re-layouts: 20.5 us -> 20.1 us
  transfers between devices with their start and end apart: 19 -> 19, of which waited for: 15 -> 14; matrix products, arithmetic and copies ran while one was open for 8% -> 8% of each run, Pallas kernels for 0% -> 0%
where the time goes in v1:
time: 891 us; the launch traced here: 881 us
  waiting for transfers between devices  295 us (33%)
  blocking collectives  250 us (28%)
  matrix products  157 us (18%)
  local copies, waits for them, and re-layouts  71.7 us (8%)
  starting transfers between devices  57.6 us (6%)
  other arithmetic  34.6 us (4%)
  between operations  15.8 us (2%)
    unnamed x1, blocking collectives  250 us
    all_to_all x1, waiting for transfers between devices, on_device(): lax.all_to_all(jnp.stack([weight[0]] * lax.axis_size('fsdp')), 'fsdp', 0, 0)  183 us
    dot_general x17, matrix products, contract_cols(): lax.dot_general(left, right, (((1,), (1,)), ((), ())), preferred_element_...  74.6 us
    dot_general x6, matrix products, project(): result = jnp.dot(flat, matrix, preferred_element_type=jnp.float32)  53.2 us
    all_gather x1, waiting for transfers between devices, on_device(): lax.all_gather(excite[0], 'fsdp', axis=0, tiled=True)  45.7 us
    ppermute x10, waiting for transfers between devices, shifted(): lax.ppermute(value, axis, [(source, source + steps) for source in range(l...  39.2 us
    ppermute x10, starting transfers between devices, shifted(): lax.ppermute(value, axis, [(source, source + steps) for source in range(l...  28.9 us
    unnamed x8, waiting for transfers between devices  27 us
  transfers between devices with their start and end apart: 19, of which 14 were waited for; matrix products, arithmetic and copies ran while one was open for 8% of the time, Pallas kernels for 0%

profile of v1, /device:TPU:42, one launch (start us, length us, event | category | flops | bytes accessed | tf_op | source)
XLA Modules:
  0.0 881.4 jit_solution(6184647605714641634)
XLA Ops:
  7.2 7.3 stack.3
  14.5 7.1 all-to-all-start
  23.1 6.0 gather_fusion
  29.1 3.4 fusion.305
  34.9 2.0 constant_dynamic-slice_fusion.56
  36.8 2.3 fusion.304
  39.1 183.4 %all-to-all-done = bf16[8,360,2880]{2,1,0:T(8,128)(2,1)} async-done(((bf16[8,360,2880]{2,1,0:T(8,128)(2,1)}), bf16[8,360,2880]{2,1,0:T(8,128)(2,1)}, u32[]{:S(2)}, u32[]{:S(2)}) %all-to-all-start) | async-done | bytes 16588832 | tf_op jit(solution)/shard_map/all_to_all | solution.py:78
  222.5 9.7 %convert_reduce_fusion.4 = (f32[2,2880]{1,0:T(2,128)S(1)}, bf16[2,49,2880]{2,1,0:T(8,128)(2,1)S(1)}, f32[2,49,2880]{2,1,0:T(8,128)}) fusion(bf16[2880,2880,1]{1,0,2:T(8,128)(2,1)} %bitcast.4, bf16[1,2,49,2880]{3,1,2,0:T(2,128)(2,1)S(1)} %get-tuple-element.33, pred[]{:T(512)S(6)} %eq.4), kind=kOutput, calls=%fused_computation.107 | convolution fusion | flops 1627954560 | bytes 18869760 | tf_op jit(solution)/shard_map/dot_general | solution.py:32
  232.2 2.0 constant_dynamic-update-slice_fusion.29
  234.2 45.7 %all-gather.7.cloned.1.call-done = bf16[1,2880,360]{2,1,0:T(8,128)(2,1)} async-done(((bf16[1,360,360]{2,1,0:T(8,128)(2,1)}), bf16[1,2880,360]{2,1,0:T(8,128)(2,1)}) %all-gather.7.cloned.1.call-update) | async-done | bytes 2073616 | tf_op jit(solution)/shard_map/all_gather | solution.py:81
  279.9 2.3 constant_dynamic-update-slice_fusion.34
  283.0 2.1 collective-permute-start
  286.7 7.3 collective-permute-done
  294.1 8.8 convert_reduce_fusion.3
  306.0 1.9 collective-permute-start.1
  311.4 5.6 collective-permute-done.1
  317.0 8.7 convert_reduce_fusion.2
  327.6 2.1 collective-permute-start.2
  332.3 6.4 collective-permute-done.2
  338.7 8.7 convert_reduce_fusion.1
  349.3 1.9 collective-permute-start.3
  353.8 6.5 collective-permute-done.3
  360.3 8.7 convert_reduce_fusion
  371.2 2.3 collective-permute-start.4
  374.6 2.0 constant_dynamic-slice_fusion.52
  376.6 5.6 collective-permute-done.4
  382.3 8.8 bitcast_dynamic-update-slice_fusion
  396.7 12.4 %fusion.5 = bf16[2,49,2880]{2,1,0:T(8,128)(2,1)} fusion(bf16[2880,2880,1]{1,0,2:T(8,128)(2,1)} %bitcast.4, bf16[1,2,49,2880]{3,1,2,0:T(2,128)(2,1)} %get-tuple-element.30, pred[]{:T(512)S(6)} %eq.5, f32[3,2,49,2880]{3,2,1,0:T(8,128)} %copy-done.9, s32[]{:T(128)S(6)} %min.30, f32[2,2880]{1,0:T(2,128)} %convolution_multiply_fusion.5, ...), kind=kOutput, calls=%fused_computation.11 | convolution fusion | flops 1630500480 | bytes 20043520 | tf_op jit(solution)/shard_map/dot_general | solution.py:25
  410.8 2.1 collective-permute-start.5
  413.8 2.1 select_dynamic-update-slice_fusion
  420.0 2.0 fusion.89
  424.3 12.4 %fusion.6 = bf16[2,49,2880]{2,1,0:T(8,128)(2,1)} fusion(bf16[2880,2880,1]{1,0,2:T(8,128)(2,1)} %bitcast.4, bf16[2,49,2880]{2,0,1:T(2,128)(2,1)} %copy-done.26, bf16[1,2,49,2880]{3,1,2,0:T(2,128)(2,1)S(1)} %copy-done.14, pred[]{:T(512)S(6)} %eq.5, f32[3,2,49,2880]{3,2,1,0:T(8,128)} %copy-done.9, s32[]{:T(128)S(6)} %min.29, ...), kind=kOutput, calls=%fused_computation.12 | convolution fusion | flops 1630500480 | bytes 21197568 | tf_op jit(solution)/shard_map/dot_general | solution.py:25
  438.3 4.0 collective-permute-start.6
  443.1 2.9 bitcast_dynamic-update-slice_fusion.10
  446.0 2.0 constant_dynamic-slice_fusion.29
  449.4 2.0 fusion.93
  453.8 12.2 %fusion.7 = bf16[2,49,2880]{2,1,0:T(8,128)(2,1)} fusion(bf16[2880,2880,1]{1,0,2:T(8,128)(2,1)} %bitcast.4, bf16[2,49,2880]{2,0,1:T(2,128)(2,1)S(1)} %copy-done.29, bf16[1,2,49,2880]{3,1,2,0:T(2,128)(2,1)S(1)} %get-tuple-element.28, pred[]{:T(512)S(6)} %eq.5, f32[3,2,49,2880]{3,2,1,0:T(8,128)} %copy-done.9, s32[]{:T(128)S(6)} %min.28, ...), kind=kOutput, calls=%fused_computation.13 | convolution fusion | flops 1630500480 | bytes 21197568 | tf_op jit(solution)/shard_map/dot_general | solution.py:25
  467.6 4.0 collective-permute-start.7
  472.3 2.9 bitcast_dynamic-update-slice_fusion.9
  475.2 2.0 constant_dynamic-slice_fusion.26
  478.6 2.0 fusion.97
  482.9 12.2 %fusion.8 = bf16[2,49,2880]{2,1,0:T(8,128)(2,1)} fusion(bf16[2880,2880,1]{1,0,2:T(8,128)(2,1)} %bitcast.4, bf16[2,49,2880]{2,0,1:T(2,128)(2,1)S(1)} %copy-done.33, bf16[1,2,49,2880]{3,1,2,0:T(2,128)(2,1)S(1)} %get-tuple-element.28, pred[]{:T(512)S(6)} %eq.5, f32[3,2,49,2880]{3,2,1,0:T(8,128)} %copy-done.9, s32[]{:T(128)S(6)} %min.27, ...), kind=kOutput, calls=%fused_computation.14 | convolution fusion | flops 1630500480 | bytes 21197568 | tf_op jit(solution)/shard_map/dot_general | solution.py:25
  496.8 4.3 collective-permute-start.8
  501.8 2.9 bitcast_dynamic-update-slice_fusion.8
  504.7 2.0 constant_dynamic-slice_fusion.23
  507.9 2.0 fusion.101
  512.2 12.2 %fusion.9 = bf16[2,49,2880]{2,1,0:T(8,128)(2,1)} fusion(bf16[2880,2880,1]{1,0,2:T(8,128)(2,1)} %bitcast.4, bf16[2,49,2880]{2,0,1:T(2,128)(2,1)S(1)} %collective-permute-done.8, bf16[1,2,49,2880]{3,1,2,0:T(2,128)(2,1)S(1)} %get-tuple-element.28, pred[]{:T(512)S(6)} %eq.5, f32[3,2,49,2880]{3,2,1,0:T(8,128)} %copy-done.9, s32[]{:T(128)S(6)} %min.26, ...), kind=kOutput, calls=%fused_computation.15 | convolution fusion | flops 1630500480 | bytes 21197568 | tf_op jit(solution)/shard_map/dot_general | solution.py:25
  526.1 4.0 collective-permute-start.9
  530.7 3.1 bitcast_dynamic-update-slice_fusion.7
  535.0 2.2 collective-permute-done.9
  537.7 2.2 fusion.4
  540.8 2.9 fusion.3
  546.0 13.9 %bitcast_convert_fusion = bf16[2880,2880]{1,0:T(8,128)(2,1)} fusion(bf16[3,2,49,2880]{3,2,1,0:T(8,128)(2,1)} %bitcast_dynamic-update-slice_fusion.11, bf16[3,2,49,2880]{3,2,1,0:T(8,128)(2,1)S(1)} %bitcast_dynamic-update-slice_fusion.6), kind=kOutput, calls=%fused_computation.1 | convolution fusion | flops 4885401600 | bytes 19975680 | tf_op jit(solution)/shard_map/dot_general | solution.py:19
  559.9 249.8 %fusion.303 = (bf16[96,2880]{1,0:T(8,128)(2,1)S(1)}, bf16[96,360]{1,0:T(8,128)(2,1)S(1)}, bf16[96,360]{1,0:T(8,128)(2,1)S(1)}) fusion(bf16[2880,2880]{1,0:T(8,128)(2,1)} %bitcast_convert_fusion, bf16[2880,360]{1,0:T(8,128)(2,1)} %fusion.3, bf16[2880,360]{1,0:T(8,128)(2,1)S(1)} %copy-done.35), kind=kCustom, calls=%all-reduce-scatter.3 | all-reduce-scatter fusion | flops 11059201 | bytes 21427712
  809.7 1.9 collective-permute-start.10
  811.8 5.6 collective-permute-start.11
  817.4 1.9 collective-permute-start.14
  819.3 2.5 collective-permute-start.15
  823.2 7.7 collective-permute-start.12
  830.8 18.0 %collective-permute-done.15 = bf16[90,360]{1,0:T(8,128)(2,1)S(1)} collective-permute-done((bf16[90,360]{1,0:T(8,128)(2,1)S(1)}, bf16[90,360]{1,0:T(8,128)(2,1)S(1)}, u32[]{:S(2)}, u32[]{:S(2)}) %collective-permute-start.15) | collective-permute-done | bytes 64832
  848.8 1.9 collective-permute-start.13
  852.3 7.6 collective-permute-done.13
  861.4 9.5 %concatenate = bf16[282,2880]{1,0:T(8,128)(2,1)} concatenate(bf16[90,2880]{1,0:T(8,128)(2,1)S(1)} %collective-permute-done.11, bf16[96,2880]{1,0:T(8,128)(2,1)S(1)} %collective-permute-done.10, bf16[96,2880]{1,0:T(8,128)(2,1)S(1)} %get-tuple-element.15), dimensions={0} | concatenate | bytes 3248640
  872.3 2.1 copy.68
  (216 shorter events, 69.6 us)
Async XLA Ops:
  7.2 16.0 %copy-start = (bf16[3,2,49,2880]{3,1,2,0:T(2,128)(2,1)S(1)}, bf16[3,2,49,2880]{3,1,2,0:T(2,128)(2,1)}, u32[]{:S(2)}) copy-start(bf16[3,2,49,2880]{3,1,2,0:T(2,128)(2,1)} %param.6) | copy-start | bytes 5080324
  14.5 8.6 copy-start.44
  14.5 208.0 %all-to-all-start = ((bf16[8,360,2880]{2,1,0:T(8,128)(2,1)}), bf16[8,360,2880]{2,1,0:T(8,128)(2,1)}, u32[]{:S(2)}, u32[]{:S(2)}) async-start(bf16[8,360,2880]{2,1,0:T(8,128)(2,1)} %stack.3), calls=%async_computation | async-start | bytes 33914880 | tf_op jit(solution)/shard_map/all_to_all | solution.py:78
  21.6 210.6 %all-gather.5.cloned.1.call-start = ((), (), s32[]{:S(2)}) async-start(), calls=%async_computation.1 | async-start | bytes 2488320 | tf_op jit(solution)/shard_map/all_gather | solution.py:80
  22.3 257.6 %all-gather.7.cloned.1.call-start = ((), (), s32[]{:S(2)}) async-start(), calls=%async_computation.2 | async-start | bytes 2488320 | tf_op jit(solution)/shard_map/all_gather | solution.py:81
  33.9 3.0 copy-start.36
  283.0 11.1 %collective-permute-start = (bf16[2,49,2880]{2,0,1:T(2,128)(2,1)S(1)}, bf16[2,49,2880]{2,0,1:T(2,128)(2,1)S(1)}, u32[]{:S(2)}, u32[]{:S(2)}) collective-permute-start(bf16[2,49,2880]{2,0,1:T(2,128)(2,1)S(1)} %copy.44), channel_id=1, source_target_pairs={{0,32},{32,64},{64,96},{1,33},{33,65},{65,97},{2,34},{34,66},{66,9... | collective-permute-start | bytes 1693448 | tf_op jit(solution)/shard_map/ppermute | solution.py:10
  285.1 1.3 copy-start.37
  286.6 7.5 copy-start.17
  294.1 8.8 %copy-start.2 = (bf16[1,2880,360]{2,1,0:T(8,128)(2,1)S(1)}, bf16[1,2880,360]{2,1,0:T(8,128)(2,1)}, u32[]{:S(2)}) copy-start(bf16[1,2880,360]{2,1,0:T(8,128)(2,1)} %all-gather.5.cloned.1.call-done) | copy-start | bytes 6220804
  302.9 1.6 copy-start.3
  306.0 11.1 %collective-permute-start.1 = (bf16[2,49,2880]{2,0,1:T(2,128)(2,1)S(1)}, bf16[2,49,2880]{2,0,1:T(2,128)(2,1)S(1)}, u32[]{:S(2)}, u32[]{:S(2)}) collective-permute-start(bf16[2,49,2880]{2,0,1:T(2,128)(2,1)S(1)} %copy.47), channel_id=1, source_target_pairs={{0,32},{32,64},{64,96},{1,33},{33,65},{65,97},{2,34},{34,66},{66,9... | collective-permute-start | bytes 1693448 | tf_op jit(solution)/shard_map/ppermute | solution.py:10
  308.1 1.1 copy-start.20
  327.6 11.1 %collective-permute-start.2 = (bf16[2,49,2880]{2,0,1:T(2,128)(2,1)S(1)}, bf16[2,49,2880]{2,0,1:T(2,128)(2,1)S(1)}, u32[]{:S(2)}, u32[]{:S(2)}) collective-permute-start(bf16[2,49,2880]{2,0,1:T(2,128)(2,1)S(1)} %copy.49), channel_id=1, source_target_pairs={{0,32},{32,64},{64,96},{1,33},{33,65},{65,97},{2,34},{34,66},{66,9... | collective-permute-start | bytes 1693448 | tf_op jit(solution)/shard_map/ppermute | solution.py:10
  349.3 11.1 %collective-permute-start.3 = (bf16[2,49,2880]{2,0,1:T(2,128)(2,1)S(1)}, bf16[2,49,2880]{2,0,1:T(2,128)(2,1)S(1)}, u32[]{:S(2)}, u32[]{:S(2)}) collective-permute-start(bf16[2,49,2880]{2,0,1:T(2,128)(2,1)S(1)} %copy.51), channel_id=1, source_target_pairs={{0,32},{32,64},{64,96},{1,33},{33,65},{65,97},{2,34},{34,66},{66,9... | collective-permute-start | bytes 1693448 | tf_op jit(solution)/shard_map/ppermute | solution.py:10
  371.2 11.1 %collective-permute-start.4 = (bf16[2,49,2880]{2,0,1:T(2,128)(2,1)S(1)}, bf16[2,49,2880]{2,0,1:T(2,128)(2,1)S(1)}, u32[]{:S(2)}, u32[]{:S(2)}) collective-permute-start(bf16[2,49,2880]{2,0,1:T(2,128)(2,1)S(1)} %copy.53), channel_id=1, source_target_pairs={{0,32},{32,64},{64,96},{1,33},{33,65},{65,97},{2,34},{34,66},{66,9... | collective-permute-start | bytes 1693448 | tf_op jit(solution)/shard_map/ppermute | solution.py:10
  376.6 14.4 %copy-start.15 = (bf16[1,2,49,2880]{3,1,2,0:T(2,128)(2,1)S(1)}, bf16[1,2,49,2880]{3,1,2,0:T(2,128)(2,1)}, u32[]{:S(2)}) copy-start(bf16[1,2,49,2880]{3,1,2,0:T(2,128)(2,1)} %get-tuple-element.30) | copy-start | bytes 1693444
  382.3 8.8 copy-start.18
  391.0 2.8 copy-start.9
  392.4 1.5 copy-start.41
  409.2 4.5 copy-start.16
  409.2 4.5 copy-start.39
  409.2 4.5 copy-start.40
  410.8 9.2 %collective-permute-start.5 = (bf16[2,49,2880]{2,0,1:T(2,128)(2,1)S(1)}, bf16[2,49,2880]{2,0,1:T(2,128)(2,1)S(1)}, u32[]{:S(2)}, u32[]{:S(2)}) collective-permute-start(bf16[2,49,2880]{2,0,1:T(2,128)(2,1)S(1)} %copy.57), channel_id=1, source_target_pairs={{32,0},{64,32},{96,64},{33,1},{65,33},{97,65},{34,2},{66,34},{98,6... | collective-permute-start | bytes 1693448 | tf_op jit(solution)/shard_map/ppermute | solution.py:10
  413.7 3.6 copy-start.19
  413.7 3.6 copy-start.21
  415.8 1.5 copy-start.11
  417.3 2.6 copy-start.13
  418.4 3.6 copy-start.4
  420.0 3.0 copy-start.26
  423.0 1.3 copy-start.14
  436.7 6.4 copy-start.22
  436.7 6.4 copy-start.27
  438.3 11.1 %collective-permute-start.6 = (bf16[2,49,2880]{2,0,1:T(2,128)(2,1)S(1)}, bf16[2,49,2880]{2,0,1:T(2,128)(2,1)S(1)}, u32[]{:S(2)}, u32[]{:S(2)}) collective-permute-start(bf16[2,49,2880]{2,0,1:T(2,128)(2,1)S(1)} %copy.60), channel_id=1, source_target_pairs={{32,0},{64,32},{96,64},{33,1},{65,33},{97,65},{34,2},{66,34},{98,6... | collective-permute-start | bytes 1693448 | tf_op jit(solution)/shard_map/ppermute | solution.py:10
  448.0 3.5 copy-start.5
  449.4 3.0 copy-start.28
  452.5 1.3 copy-start.29
  466.0 6.3 copy-start.23
  467.6 11.0 %collective-permute-start.7 = (bf16[2,49,2880]{2,0,1:T(2,128)(2,1)S(1)}, bf16[2,49,2880]{2,0,1:T(2,128)(2,1)S(1)}, u32[]{:S(2)}, u32[]{:S(2)}) collective-permute-start(bf16[2,49,2880]{2,0,1:T(2,128)(2,1)S(1)} %copy.62), channel_id=1, source_target_pairs={{32,0},{64,32},{96,64},{33,1},{65,33},{97,65},{34,2},{66,34},{98,6... | collective-permute-start | bytes 1693448 | tf_op jit(solution)/shard_map/ppermute | solution.py:10
  477.2 3.5 copy-start.6
  478.6 3.0 copy-start.32
  481.6 1.3 copy-start.33
  495.1 6.6 copy-start.25
  495.1 6.6 copy-start.34
  496.8 11.1 %collective-permute-start.8 = (bf16[2,49,2880]{2,0,1:T(2,128)(2,1)S(1)}, bf16[2,49,2880]{2,0,1:T(2,128)(2,1)S(1)}, u32[]{:S(2)}, u32[]{:S(2)}) collective-permute-start(bf16[2,49,2880]{2,0,1:T(2,128)(2,1)S(1)} %copy.64), channel_id=1, source_target_pairs={{32,0},{64,32},{96,64},{33,1},{65,33},{97,65},{34,2},{66,34},{98,6... | collective-permute-start | bytes 1693448 | tf_op jit(solution)/shard_map/ppermute | solution.py:10
  506.7 3.3 copy-start.7
  507.9 4.3 copy-start.30
  524.4 6.3 copy-start.24
  524.4 6.3 copy-start.31
  526.1 11.1 %collective-permute-start.9 = (bf16[2,49,2880]{2,0,1:T(2,128)(2,1)S(1)}, bf16[2,49,2880]{2,0,1:T(2,128)(2,1)S(1)}, u32[]{:S(2)}, u32[]{:S(2)}) collective-permute-start(bf16[2,49,2880]{2,0,1:T(2,128)(2,1)S(1)} %copy.66), channel_id=1, source_target_pairs={{32,0},{64,32},{96,64},{33,1},{65,33},{97,65},{34,2},{66,34},{98,6... | collective-permute-start | bytes 1693448 | tf_op jit(solution)/shard_map/ppermute | solution.py:10
  530.7 6.4 copy-start.10
  534.9 2.8 copy-start.42
  537.7 2.2 copy-start.8
  537.7 2.2 copy-start.38
  543.7 1.5 copy-start.12
  546.0 13.9 %copy-start.35 = (bf16[2880,360]{1,0:T(8,128)(2,1)S(1)}, bf16[2880,360]{1,0:T(8,128)(2,1)}, u32[]{:S(2)}) copy-start(bf16[2880,360]{1,0:T(8,128)(2,1)} %fusion.4) | copy-start | bytes 6220804
  559.9 262.0 %copy-start.43 = (u32[128]{0:T(128)S(1)}, u32[128]{0:T(128)}, u32[]{:S(2)}) copy-start(u32[128]{0:T(128)} %constant.371) | copy-start | bytes 1540
  809.7 51.7 %collective-permute-start.10 = (bf16[96,2880]{1,0:T(8,128)(2,1)S(1)}, bf16[96,2880]{1,0:T(8,128)(2,1)S(1)}, u32[]{:S(2)}, u32[]{:S(2)}) collective-permute-start(bf16[96,2880]{1,0:T(8,128)(2,1)S(1)} %get-tuple-element.15), channel_id=1, source_target_pairs={{0,1},{1,2},{2,3},{3,4},{4,5},{5,6},{6,7},{7,8},{8,9},{9,10},{10,1... | collective-permute-start | bytes 1658888
  811.8 49.6 %collective-permute-start.11 = (bf16[90,2880]{1,0:T(8,128)(2,1)S(1)}, bf16[90,2880]{1,0:T(8,128)(2,1)S(1)}, u32[]{:S(2)}, u32[]{:S(2)}) collective-permute-start(bf16[90,2880]{1,0:T(8,128)(2,1)S(1)} %slice.35), channel_id=1, source_target_pairs={{0,2},{1,3},{2,4},{3,5},{4,6},{5,7},{6,8},{7,9},{8,10},{9,11},{10,... | collective-permute-start | bytes 1555208
  817.4 33.4 %collective-permute-start.14 = (bf16[96,360]{1,0:T(8,128)(2,1)S(1)}, bf16[96,360]{1,0:T(8,128)(2,1)S(1)}, u32[]{:S(2)}, u32[]{:S(2)}) collective-permute-start(bf16[96,360]{1,0:T(8,128)(2,1)S(1)} %get-tuple-element.17), channel_id=1, source_target_pairs={{0,1},{1,2},{2,3},{3,4},{4,5},{5,6},{6,7},{7,8},{8,9},{9,10},{10,1... | collective-permute-start | bytes 207368
  819.3 29.5 %collective-permute-start.15 = (bf16[90,360]{1,0:T(8,128)(2,1)S(1)}, bf16[90,360]{1,0:T(8,128)(2,1)S(1)}, u32[]{:S(2)}, u32[]{:S(2)}) collective-permute-start(bf16[90,360]{1,0:T(8,128)(2,1)S(1)} %slice.37), channel_id=1, source_target_pairs={{0,2},{1,3},{2,4},{3,5},{4,6},{5,7},{6,8},{7,9},{8,10},{9,11},{10,... | collective-permute-start | bytes 194408
  823.2 36.7 %collective-permute-start.12 = (bf16[96,360]{1,0:T(8,128)(2,1)S(1)}, bf16[96,360]{1,0:T(8,128)(2,1)S(1)}, u32[]{:S(2)}, u32[]{:S(2)}) collective-permute-start(bf16[96,360]{1,0:T(8,128)(2,1)S(1)} %get-tuple-element.16), channel_id=1, source_target_pairs={{0,1},{1,2},{2,3},{3,4},{4,5},{5,6},{6,7},{7,8},{8,9},{9,10},{10,1... | collective-permute-start | bytes 207368
  848.8 11.0 %collective-permute-start.13 = (bf16[90,360]{1,0:T(8,128)(2,1)S(1)}, bf16[90,360]{1,0:T(8,128)(2,1)S(1)}, u32[]{:S(2)}, u32[]{:S(2)}) collective-permute-start(bf16[90,360]{1,0:T(8,128)(2,1)S(1)} %slice.36), channel_id=1, source_target_pairs={{0,2},{1,3},{2,4},{3,5},{4,6},{5,7},{6,8},{7,9},{8,10},{9,11},{10,... | collective-permute-start | bytes 194408
  871.0 3.4 copy-start.1
Sparse Core Ops, SparseCore 0:
  24.7 201.0 all-gather.4
  228.2 51.7 all-gather.6
